TPU v7x, 32 devices: a whole 2x2x4 slice. The times are simulated.
32 devices in a mesh: ctx: 4 (over z), ep: 8 (over y, x, core).
Axes of the slice: x: 2, y: 2, z: 4, core: 2. Of those that a mesh axis runs over, the one named last changes fastest.
Arguments:
- hidden_in: bfloat16 [8, 512, 7168], P('ep', None, 'ctx'), may hold values from -6 to 6
- expert_ids: int32 [8, 512, 1], P('ep'), may hold values from 0 to 3; in each aligned block of 512 rows (0 to 511, 512 to 1023, ..., all dimensions but the last counted through in order) at most 192 rows name the same one
- route_weight: float32 [8, 512, 1], P('ep'), may hold values from 0.05 to 1
- w_gate: bfloat16 [7168, 4096], P('ctx', 'ep'), may hold values from -0.0625 to 0.0625
- w_up: bfloat16 [7168, 4096], P('ctx', 'ep'), may hold values from -0.0625 to 0.0625
- w_down: bfloat16 [4096, 7168], P('ep', 'ctx'), may hold values from -0.1875 to 0.1875
- queries: bfloat16 [8, 512, 6912], P('ep', 'ctx'), may hold values from -112 to 112
- latents: bfloat16 [8, 512, 512], P('ep', 'ctx'), may hold values from -5 to 5
- rope_keys: bfloat16 [8, 512, 64], P('ep', 'ctx'), may hold values from -5 to 5
- marks: int32 [8, 512], P('ep', 'ctx'), may hold values from 0 to 1, as said below
Outputs:
- moe_out: bfloat16 [8, 512, 7168], P('ep', None, 'ctx')
- context: bfloat16 [8, 512, 6144], P('ep', 'ctx')
Inputs may be any that keep to these rules, and one draw needn't show every extreme that they name: `expert_ids`: in each sequence no expert is named by more than 192 pairs; in some sequences one is named by exactly 192. `marks`: in each sequence the positions marked 1 form one run of consecutive positions, all in the first half.
All inputs are finite; a program needn't handle non-finite values.
Results may differ from a plain program's by a relative error of at most 0.02.
Values may be sent and summed in bfloat16 or wider, within the bound.
A program may use at most 128 MiB of HBM per device.

v0:
```python
import math

import jax
import jax.numpy as jnp
from jax import lax
from jax.sharding import PartitionSpec as P

LAT = 512
ROPE = 64
QK_DIM = 192


def attend_rows(query_rows_all, query_pos, latents, rope_keys, marks):
    query_rows = query_rows_all.shape[0]
    heads = query_rows_all.shape[1] // (LAT + ROPE)
    query_heads = query_rows_all.reshape(query_rows, heads, LAT + ROPE)
    query_lat = query_heads[:, :, :LAT]
    query_rot = query_heads[:, :, LAT:]
    scale = 1.0 / math.sqrt(QK_DIM)
    marks_wire = marks.astype(jnp.bfloat16)
    latent_piece = lax.all_gather(latents, "ctx", axis=1, tiled=True)[0]
    rope_piece = lax.all_gather(rope_keys, "ctx", axis=1, tiled=True)[0]
    mark_piece = lax.all_gather(marks_wire, "ctx", axis=1, tiled=True)[0]
    count = latent_piece.shape[0]
    key_pos = jnp.arange(count, dtype=jnp.int32)
    running_top = jnp.full((heads, query_rows), -1e30, jnp.float32)
    scores = jnp.einsum("qhd,kd->hqk", query_lat, latent_piece, preferred_element_type=jnp.float32)
    scores = scores + jnp.einsum(
        "qhd,kd->hqk", query_rot, rope_piece, preferred_element_type=jnp.float32
    )
    scores = scores * scale
    own_key = key_pos[None, :] == query_pos[:, None]
    visible = (key_pos[None, :] <= query_pos[:, None]) & ((mark_piece[None, :] < 0.5) | own_key)
    masked = jnp.where(visible[None], scores, -1e30)
    new_top = jnp.maximum(running_top, jnp.max(masked, axis=-1))
    weights = jnp.where(visible[None], jnp.exp(masked - new_top[:, :, None]), 0.0)
    new_total = jnp.sum(weights, axis=-1)
    weights_b = weights.astype(jnp.bfloat16)
    new_acc = jnp.einsum("hqk,kd->hqd", weights_b, latent_piece, preferred_element_type=jnp.float32)
    result = new_acc / new_total[:, :, None]
    result = jnp.transpose(result, (1, 0, 2)).reshape(query_rows, heads * LAT)
    return result.astype(jnp.bfloat16)


def attend(queries, latents, rope_keys, marks):
    query_rows = queries.shape[1]
    me_index = lax.axis_index("ctx")
    query_pos = me_index * query_rows + jnp.arange(query_rows, dtype=jnp.int32)
    return attend_rows(queries[0], query_pos, latents, rope_keys, marks)[None]


def expert_rows(rows, w_gate, w_up, w_down):
    gate_part = jnp.dot(rows, w_gate, preferred_element_type=jnp.float32)
    up_part = jnp.dot(rows, w_up, preferred_element_type=jnp.float32)
    gate_act, up_act = (
        lax.psum(gate_part.astype(jnp.bfloat16), "ctx").astype(jnp.float32),
        lax.psum(up_part.astype(jnp.bfloat16), "ctx").astype(jnp.float32),
    )
    hidden = (jax.nn.silu(gate_act) * up_act).astype(jnp.bfloat16)
    return jnp.dot(hidden, w_down, preferred_element_type=jnp.float32).astype(jnp.bfloat16)


def mixture(hidden_in, expert_ids, route_weight, w_gate, w_up, w_down):
    features = hidden_in[0]
    seq_len = features.shape[0]
    width_part = features.shape[1]
    routed = expert_ids[0]
    slots_per = routed.shape[1]
    experts = lax.axis_size("ep") // 2
    capacity = max(2, 3 * seq_len * slots_per // (2 * experts))
    flat_ids = routed.reshape(-1)
    onehot = (flat_ids[:, None] == jnp.arange(experts, dtype=jnp.int32)[None, :]).astype(jnp.int32)
    rank = jnp.sum(jnp.cumsum(onehot, axis=0) * onehot, axis=1) - 1
    slot = flat_ids * capacity + rank
    packed = jnp.zeros((experts * capacity, width_part), jnp.bfloat16).at[slot].set(features)
    outbound = jnp.broadcast_to(
        packed.reshape(experts, 1, capacity, width_part), (experts, 2, capacity, width_part)
    )
    outbound = outbound.reshape(2 * experts, capacity, width_part)
    inbound = lax.all_to_all(outbound, "ep", split_axis=0, concat_axis=0, tiled=True)
    produced = expert_rows(inbound.reshape(-1, width_part), w_gate, w_up, w_down)
    back = lax.all_to_all(
        produced.reshape(2 * experts, capacity, width_part),
        "ep",
        split_axis=0,
        concat_axis=0,
        tiled=True,
    )
    halves = back.reshape(experts, 2, capacity, width_part).astype(jnp.float32)
    combined = (halves[:, 0] + halves[:, 1]).reshape(experts * capacity, width_part)
    picked = jnp.take(combined, slot, axis=0).reshape(seq_len, slots_per, width_part)
    weighted = jnp.sum(picked * route_weight[0][:, :, None], axis=1)
    return weighted.astype(jnp.bfloat16)[None]


def per_device(
    hidden_in, expert_ids, route_weight, w_gate, w_up, w_down, queries, latents, rope_keys, marks
):
    context = attend(queries, latents, rope_keys, marks)
    moe_out = mixture(hidden_in, expert_ids, route_weight, w_gate, w_up, w_down)
    return (moe_out, context)


def solution(mesh):
    placed = (
        P("ep", None, "ctx"),
        P("ep", None, None),
        P("ep", None, None),
        P("ctx", "ep"),
        P("ctx", "ep"),
        P("ep", "ctx"),
        P("ep", "ctx", None),
        P("ep", "ctx", None),
        P("ep", "ctx", None),
        P("ep", "ctx"),
    )
    return jax.shard_map(
        per_device,
        mesh=mesh,
        in_specs=placed,
        out_specs=(P("ep", None, "ctx"), P("ep", "ctx", None)),
        check_vma=False,
    )
```

profile of v0, /device:TPU:0, one launch (start us, length us, event | category | flops | bytes accessed | tf_op | source)
XLA Modules:
  0.0 317.2 jit_solution(17324685447485344345)
XLA Ops:
  7.2 0.0 copy-start
  7.2 0.0 all-reduce.3.cloned.1.call-start
  7.2 0.8 fusion.30
  8.0 1.2 reduce-window.6
  9.2 0.2 slice_reduce_fusion
  9.5 0.2 reduce-window.9
  9.6 0.1 add_bitcast_fusion
  9.7 0.7 fusion.29
  10.4 0.7 compare_select_fusion
  11.1 6.1 %scatter_custom_fusion = bf16[768,1792]{1,0:T(8,128)(2,1)} fusion(s32[512]{0:T(512)S(1)} %bitcast.87, bf16[1,512,1792]{2,1,0:T(8,128)(2,1)} %param.10, bf16[]{:T(256)} %constant.20.clone.1), kind=kCustom, calls=%fused_computation.24 | custom fusion | bytes 4587522 | tf_op jit(solution)/shard_map/scatter | solution.py:75
  17.3 2.2 broadcast_in_dim.56
  19.4 0.0 copy-start.6
  19.4 68.2 %all_to_all.10 = bf16[8,192,1792]{2,1,0:T(8,128)(2,1)S(1)} all-to-all(bf16[8,192,1792]{2,1,0:T(8,128)(2,1)S(1)} %bitcast.75), channel_id=1, replica_groups=mesh['ctx'=4,'ep'=8] {'ep'}, dimensions={0} | all-to-all | bytes 11010048 | tf_op jit(solution)/shard_map/all_to_all | solution.py:80
  87.7 0.0 copy-done.6
  87.7 0.0 copy-start.7
  87.7 4.1 %convolution_convert_fusion.1 = bf16[1536,512]{1,0:T(8,128)(2,1)} fusion(bf16[1536,1792]{1,0:T(8,128)(2,1)S(1)} %bitcast.81, bf16[1792,512]{1,0:T(8,128)(2,1)S(1)} %copy-done.6), kind=kOutput, calls=%fused_computation.20 | convolution fusion | flops 2819358720 | bytes 8912896 | tf_op jit(solution)/shard_map/dot_general | solution.py:54
  91.7 0.0 copy-done.7
  91.7 4.0 %convolution_convert_fusion.2 = bf16[1536,512]{1,0:T(8,128)(2,1)} fusion(bf16[1536,1792]{1,0:T(8,128)(2,1)S(1)} %bitcast.82, bf16[1792,512]{1,0:T(8,128)(2,1)S(1)} %copy-done.7), kind=kOutput, calls=%fused_computation.21 | convolution fusion | flops 2819358720 | bytes 8912896 | tf_op jit(solution)/shard_map/dot_general | solution.py:53
  95.8 0.0 all-reduce.3.cloned.1.call-update
  95.8 121.0 %all-reduce.3.cloned.1.call-done = (bf16[1536,512]{1,0:T(8,128)(2,1)}, bf16[1536,512]{1,0:T(8,128)(2,1)}) async-done(((bf16[1536,512]{1,0:T(8,128)(2,1)}, bf16[1536,512]{1,0:T(8,128)(2,1)}), (bf16[1536,512]{1,0:T(8,128)(2,1)}, bf16[1536,512]{1,0:T(8,128)(2,1)})) %all-reduce.3.cloned.1.call-update) | async-done | bytes 3145744 | tf_op jit(solution)/shard_map/psum | solution.py:57
  216.7 0.0 copy-done
  216.7 7.6 %convolution_convert_fusion = bf16[1536,1792]{1,0:T(8,128)(2,1)} fusion(bf16[512,1792]{1,0:T(8,128)(2,1)S(1)} %copy-done, bf16[1536,512]{1,0:T(8,128)(2,1)} %get-tuple-element.4, bf16[1536,512]{1,0:T(8,128)(2,1)} %get-tuple-element.5), kind=kOutput, calls=%fused_computation.2 | convolution fusion | flops 2827616256 | bytes 10485760 | tf_op jit(solution)/shard_map/dot_general | solution.py:60
  224.4 4.8 %all-to-all-start.1 = ((bf16[8,192,1792]{2,1,0:T(8,128)(2,1)}), bf16[8,192,1792]{2,1,0:T(8,128)(2,1)}, u32[]{:S(2)}, u32[]{:S(2)}) async-start(bf16[8,192,1792]{2,1,0:T(8,128)(2,1)} %bitcast.80), calls=%async_computation.1 | async-start | bytes 11010048 | tf_op jit(solution)/shard_map/all_to_all | solution.py:82
  229.2 0.0 copy-start.4
  229.2 0.0 copy-start.2
  229.3 0.0 copy-done.8
  229.3 2.8 copy.18
  232.1 8.6 %all_gather.9 = bf16[1,512]{1,0:T(2,128)(2,1)S(1)} all-gather(bf16[1,128]{1,0:T(2,128)(2,1)S(1)} %convert_element_type.68), channel_id=1, replica_groups=mesh['ctx'=4,'ep'=8] {'ctx'}, dimensions={1}, use_global_device_ids=true | all-gather | bytes 1280 | tf_op jit(solution)/shard_map/all_gather | solution.py:23
  240.7 0.0 copy-done.4
  240.7 12.1 %all_gather.11 = bf16[1,512,64]{1,2,0:T(8,128)(2,1)S(1)} all-gather(bf16[1,128,64]{1,2,0:T(8,128)(2,1)S(1)} %copy-done.4), channel_id=1, replica_groups=mesh['ctx'=4,'ep'=8] {'ctx'}, dimensions={1}, use_global_device_ids=true | all-gather | bytes 81920 | tf_op jit(solution)/shard_map/all_gather | solution.py:22
  252.8 0.0 copy-done.2
  252.8 15.2 %all_gather.10 = bf16[1,512,512]{2,1,0:T(8,128)(2,1)S(1)} all-gather(bf16[1,128,512]{2,1,0:T(8,128)(2,1)S(1)} %copy-done.2), channel_id=1, replica_groups=mesh['ctx'=4,'ep'=8] {'ctx'}, dimensions={1}, use_global_device_ids=true | all-gather | bytes 655360 | tf_op jit(solution)/shard_map/all_gather | solution.py:21
  268.0 0.1 fusion.23
  268.1 0.6 fusion.25
  268.7 1.1 fusion.33
  269.8 0.5 fusion.9
  270.4 1.1 fusion.7
  271.5 0.0 copy-start.3
  271.5 0.9 copy.21
  272.4 1.6 copy.22
  274.0 0.0 copy-done.3
  274.0 18.4 %all-to-all-done.1 = bf16[8,192,1792]{2,1,0:T(8,128)(2,1)} async-done(((bf16[8,192,1792]{2,1,0:T(8,128)(2,1)}), bf16[8,192,1792]{2,1,0:T(8,128)(2,1)}, u32[]{:S(2)}, u32[]{:S(2)}) %all-to-all-start.1) | async-done | bytes 5505056 | tf_op jit(solution)/shard_map/all_to_all | solution.py:82
  292.4 3.5 %convert.1 = f32[4,2,192,1792]{3,2,1,0:T(8,128)S(1)} convert(bf16[4,2,192,1792]{3,2,1,0:T(8,128)(2,1)} %bitcast.12) | non-fusion elementwise | flops 2752512 | bytes 16515072 | tf_op jit(solution)/shard_map/convert_element_type | solution.py:89
  296.0 3.0 fusion
  299.0 7.7 %gather_fusion = f32[512,1792]{1,0:T(8,128)} fusion(f32[768,1792]{1,0:T(8,128)} %bitcast.74, s32[1024]{0:T(1024)S(1)} %pad_clamp_fusion), kind=kCustom, calls=%fused_computation | custom fusion | bytes 7342080 | tf_op jit(solution)/shard_map/jit(_take)/gather | solution.py:91
  306.7 0.0 copy-done.5
  306.7 3.7 %fusion.2 = bf16[1,512,1792]{2,1,0:T(8,128)(2,1)} fusion(f32[512,1792]{1,0:T(8,128)} %gather_fusion, f32[512]{0:T(512)S(1)} %bitcast.91, pred[512]{0:T(512)(128)(4,1)S(1)} %compare_and_fusion), kind=kLoop, calls=%fused_computation.10 | loop fusion | flops 2752512 | bytes 5507584 | tf_op jit(solution)/shard_map/convert_element_type | solution.py:93
  310.4 0.0 copy-done.1
  (10 shorter events, 0.1 us)
Async XLA Ops:
  7.2 209.6 %copy-start = (bf16[512,1792]{1,0:T(8,128)(2,1)S(1)}, bf16[512,1792]{1,0:T(8,128)(2,1)}, u32[]{:S(2)}) copy-start(bf16[512,1792]{1,0:T(8,128)(2,1)} %param.15) | copy-start | bytes 5505028
  7.2 209.6 %all-reduce.3.cloned.1.call-start = ((), (), s32[]{:S(2)}) async-start(), calls=%async_computation.2 | async-start | bytes 6291456 | tf_op jit(solution)/shard_map/psum | solution.py:57
  19.4 68.2 %copy-start.6 = (bf16[1792,512]{1,0:T(8,128)(2,1)S(1)}, bf16[1792,512]{1,0:T(8,128)(2,1)}, u32[]{:S(2)}) copy-start(bf16[1792,512]{1,0:T(8,128)(2,1)} %param.14) | copy-start | bytes 5505028
  87.7 4.1 %copy-start.7 = (bf16[1792,512]{1,0:T(8,128)(2,1)S(1)}, bf16[1792,512]{1,0:T(8,128)(2,1)}, u32[]{:S(2)}) copy-start(bf16[1792,512]{1,0:T(8,128)(2,1)} %param.13) | copy-start | bytes 5505028
  224.4 4.9 %copy-start.8 = (s32[1,128]{1,0:T(1,128)S(1)}, s32[1,128]{1,0:T(1,128)}, u32[]{:S(2)}) copy-start(s32[1,128]{1,0:T(1,128)} %param.19) | copy-start | bytes 1540
  224.4 68.0 %all-to-all-start.1 = ((bf16[8,192,1792]{2,1,0:T(8,128)(2,1)}), bf16[8,192,1792]{2,1,0:T(8,128)(2,1)}, u32[]{:S(2)}, u32[]{:S(2)}) async-start(bf16[8,192,1792]{2,1,0:T(8,128)(2,1)} %bitcast.80), calls=%async_computation.1 | async-start | bytes 11010048 | tf_op jit(solution)/shard_map/all_to_all | solution.py:82
  229.2 11.4 %copy-start.4 = (bf16[1,128,64]{1,2,0:T(8,128)(2,1)S(1)}, bf16[1,128,64]{1,2,0:T(8,128)(2,1)}, u32[]{:S(2)}) copy-start(bf16[1,128,64]{1,2,0:T(8,128)(2,1)} %param.18) | copy-start | bytes 49156
  229.2 23.5 %copy-start.2 = (bf16[1,128,512]{2,1,0:T(8,128)(2,1)S(1)}, bf16[1,128,512]{2,1,0:T(8,128)(2,1)}, u32[]{:S(2)}) copy-start(bf16[1,128,512]{2,1,0:T(8,128)(2,1)} %param.17) | copy-start | bytes 393220
  271.5 2.5 copy-start.3
  299.0 7.7 %copy-start.5 = (f32[1,512,1]{1,2,0:T(1,128)S(1)}, f32[1,512,1]{1,2,0:T(1,128)}, u32[]{:S(2)}) copy-start(f32[1,512,1]{1,2,0:T(1,128)} %param.12) | copy-start | bytes 6148
  299.0 11.4 %copy-start.1 = (bf16[512,1792]{1,0:T(8,128)(2,1)S(1)}, bf16[512,1792]{1,0:T(8,128)(2,1)}, u32[]{:S(2)}) copy-start(bf16[512,1792]{1,0:T(8,128)(2,1)} %param.15) | copy-start | bytes 5505028
Sparse Core Ops, SparseCore 0:
  95.9 120.7 all-reduce.2
where the time goes:
time: 318 us; the launch traced here: 317 us
  waiting for transfers between devices  139 us (44%)
  blocking collectives  104 us (33%)
  local copies, waits for them, and re-layouts  21.5 us (7%)
  matrix products  18.5 us (6%)
  other arithmetic  14.7 us (5%)
  between operations  14.2 us (4%)
  starting transfers between devices  4.87 us (2%)
    psum x1, waiting for transfers between devices, expert_rows(): lax.psum(up_part.astype(jnp.bfloat16), 'ctx').astype(jnp.float32)  121 us
    all_to_all x1, blocking collectives, mixture(): lax.all_to_all(outbound, 'ep', split_axis=0, concat_axis=0, tiled=True)  68.2 us
    all_to_all x1, waiting for transfers between devices, mixture(): lax.all_to_all(produced.reshape(2 * experts, capacity, width_part), 'ep',...  18.4 us
    all_gather x1, blocking collectives, attend_rows(): latent_piece = lax.all_gather(latents, 'ctx', axis=1, tiled=True)[0]  15.2 us
    all_gather x1, blocking collectives, attend_rows(): rope_piece = lax.all_gather(rope_keys, 'ctx', axis=1, tiled=True)[0]  12.1 us
    all_gather x1, blocking collectives, attend_rows(): mark_piece = lax.all_gather(marks_wire, 'ctx', axis=1, tiled=True)[0]  8.57 us
    gather x1, local copies, waits for them, and re-layouts, mixture(): jnp.take(combined, slot, axis=0).reshape(seq_len, slots_per, width_part)  7.7 us
    dot_general x1, matrix products, expert_rows(): jnp.dot(hidden, w_down, preferred_element_type=jnp.float32)  7.64 us
  transfers between devices with their start and end apart: 2, of which 2 were waited for; matrix products, arithmetic and copies ran while one was open for 3% of the time, Pallas kernels for 0%

commit v1 on v0

v1 whole, which is shorter than its diff:
```python
import functools
import math

import jax
import jax.numpy as jnp
from jax import lax
from jax.experimental import pallas as pl
from jax.experimental.pallas import tpu as pltpu
from jax.sharding import PartitionSpec as P

LAT = 512
ROPE = 64
QK_DIM = 192
CHUNKS = 8
MESH = pl.DeviceIdType.MESH


def flip(a, b, size):
    out = 0
    step = 1
    while step < size:
        out = out + lax.rem(lax.div(a, step) + lax.div(b, step), 2) * step
        step *= 2
    return out


def expert_kernel(
    chips,
    depth,
    cap,
    group,
    slot_ref,
    feat_ref,
    gate_ref,
    up_ref,
    down_ref,
    kv_ref,
    ret_ref,
    gat_ref,
    packed,
    rows,
    part_out,
    part_in,
    hid,
    half_out,
    half_in,
    summed,
    d_send,
    d_recv,
    f_send,
    f_recv,
    c_send,
    c_recv,
    b_send,
    b_recv,
    h_send,
    h_recv,
    r_send,
    r_recv,
    g_send,
    g_recv,
    l_sem,
):
    me = lax.axis_index("ep")
    z = lax.axis_index("ctx")
    core = lax.rem(me, 2)
    chip = lax.div(me, 2)
    sibling = me + 1 - 2 * core
    width = feat_ref.shape[1]
    hidden = gate_ref.shape[1]
    quarter = hidden // 2
    n = CHUNKS
    block_rows = group * cap

    def block(buf, source):
        if group == 1:
            return buf.at[source]
        start = pl.multiple_of(lax.rem(source, group) * cap, cap)
        return buf.at[lax.div(source, group), pl.ds(start, cap)]

    def remote(src, dst, send, recv, **device):
        return pltpu.make_async_remote_copy(
            src_ref=src, dst_ref=dst, send_sem=send, recv_sem=recv,
            device_id=device, device_id_type=MESH,
        )

    def dispatch(j):
        return remote(packed.at[j], block(rows, me), d_send.at[j], d_recv.at[chip], ep=2 * j + core)

    def arrival(j):
        return remote(packed.at[j], block(rows, 2 * j + core), d_send.at[j], d_recv.at[j], ep=2 * j + core)

    def forward(s):
        j = lax.div(s, 2)
        return remote(block(rows, s), block(rows, s), f_send.at[j], f_recv.at[j], ep=sibling)

    nexts = (z + 1, z - 1)
    prevs = (z - 1, z + 1)
    places = (z, depth - 1 - z)

    def chain(d, t):
        at = d * n + t
        return remote(part_out.at[at], part_in.at[at], c_send.at[at], c_recv.at[at], ctx=nexts[d])

    def spread(d, t):
        at = d * n + t
        return remote(hid.at[at], hid.at[at], b_send.at[at], b_recv.at[at], ctx=prevs[d])

    def swap(s):
        j = lax.div(s, 2)
        return remote(block(half_out, s), half_in.at[j], h_send.at[j], h_recv.at[j], ep=sibling)

    def back(j):
        return remote(summed.at[j], ret_ref.at[chip], r_send.at[j], r_recv.at[chip], ep=2 * j + core)

    def home(j):
        return remote(summed.at[j], ret_ref.at[j], r_send.at[j], r_recv.at[j], ep=2 * j + core)

    def share(o):
        other = lax.rem(z + o, depth)
        return remote(kv_ref, gat_ref.at[z], g_send.at[o], g_recv.at[o], ctx=other)

    def shared(o):
        other = lax.rem(z + depth - o, depth)
        return remote(kv_ref, gat_ref.at[other], g_send.at[o], g_recv.at[o], ctx=other)

    barrier = pltpu.get_barrier_semaphore()

    def greet(o, carry):
        pl.semaphore_signal(
            barrier, inc=1, device_id={"ep": 2 * flip(chip, o, chips) + core}, device_id_type=MESH
        )
        return carry

    lax.fori_loop(1, chips, greet, 0)
    pl.semaphore_signal(barrier, inc=1, device_id={"ep": sibling}, device_id_type=MESH)
    for o in range(1, depth):
        pl.semaphore_signal(
            barrier, inc=1, device_id={"ctx": lax.rem(z + o, depth)}, device_id_type=MESH
        )
    pl.semaphore_wait(barrier, chips + depth - 1)

    own_kv = pltpu.make_async_copy(kv_ref, gat_ref.at[z], l_sem.at[0])
    own_kv.start()

    slots = slot_ref[...]
    tokens = slots.shape[1]

    def pack(o, carry):
        j = flip(chip, o, chips)
        index = j * cap + lax.broadcasted_iota(jnp.int32, (cap, tokens), 0)
        pick = jnp.where(index == slots, 1.0, 0.0).astype(jnp.bfloat16)
        chosen = jnp.dot(pick, feat_ref[...], preferred_element_type=jnp.float32)
        packed[j] = chosen.astype(jnp.bfloat16)

        @pl.when(o < chips)
        def _():
            dispatch(j).start()

        return carry

    lax.fori_loop(1, chips, pack, 0)
    index = chip * cap + lax.broadcasted_iota(jnp.int32, (cap, tokens), 0)
    pick = jnp.where(index == slots, 1.0, 0.0).astype(jnp.bfloat16)
    chosen = jnp.dot(pick, feat_ref[...], preferred_element_type=jnp.float32)
    block(rows, me)[...] = chosen.astype(jnp.bfloat16)

    first = lax.div(me, group)
    lag = depth - 1

    def step(i, carry):
        @pl.when(i < n)
        def _():
            q = flip(first, i, n)
            for g in range(group):
                s = q * group + g
                j = lax.div(s, 2)
                mine = lax.rem(s, 2) == core

                @pl.when(mine & (j != chip))
                def _():
                    arrival(j).wait_recv()

                @pl.when(mine)
                def _():
                    forward(s).start()

            for g in range(group):
                s = q * group + g

                @pl.when(lax.rem(s, 2) != core)
                def _():
                    forward(s).wait_recv()

        for d in range(2):
            t = i - places[d]
            lo, hi = d * quarter, (d + 1) * quarter

            @pl.when((t >= 0) & (t < n))
            def _():
                q = flip(first, t, n)
                at = d * n + t
                x = rows[q]
                gate = jnp.dot(x, gate_ref[:, lo:hi], preferred_element_type=jnp.float32)
                up = jnp.dot(x, up_ref[:, lo:hi], preferred_element_type=jnp.float32)

                @pl.when(places[d] == 0)
                def _():
                    part_out[at, :, :quarter] = gate.astype(jnp.bfloat16)
                    part_out[at, :, quarter:] = up.astype(jnp.bfloat16)
                    chain(d, t).start()

                @pl.when(places[d] > 0)
                def _():
                    chain(d, t).wait_recv()
                    gate_sum = gate + part_in[at, :, :quarter].astype(jnp.float32)
                    up_sum = up + part_in[at, :, quarter:].astype(jnp.float32)

                    @pl.when(places[d] < depth - 1)
                    def _():
                        part_out[at, :, :quarter] = gate_sum.astype(jnp.bfloat16)
                        part_out[at, :, quarter:] = up_sum.astype(jnp.bfloat16)
                        chain(d, t).start()

                    @pl.when(places[d] == depth - 1)
                    def _():
                        hid[at] = (jax.nn.silu(gate_sum) * up_sum).astype(jnp.bfloat16)
                        spread(d, t).start()

        for d in range(2):
            t = i - lag - (depth - 1 - places[d])

            @pl.when((t >= 0) & (t < n) & (places[d] < depth - 1))
            def _():
                spread(d, t).wait_recv()

                @pl.when(places[d] > 0)
                def _():
                    spread(d, t).start()

        t = i - 2 * lag

        @pl.when((t >= 0) & (t < n))
        def _():
            q = flip(first, t, n)
            h0 = hid[t]
            h1 = hid[n + t]
            tile = 256
            for w in range(0, width, tile):
                got = jnp.dot(h0, down_ref[:quarter, w:w + tile], preferred_element_type=jnp.float32)
                got = got + jnp.dot(
                    h1, down_ref[quarter:, w:w + tile], preferred_element_type=jnp.float32
                )
                half_out[q, :, w:w + tile] = got.astype(jnp.bfloat16)
            for g in range(group):
                s = q * group + g

                @pl.when(lax.rem(s, 2) != core)
                def _():
                    swap(s).start()

        t2 = i - 2 * lag - 1

        @pl.when((t2 >= 0) & (t2 < n))
        def _():
            q = flip(first, t2, n)
            for g in range(group):
                s = q * group + g
                j = lax.div(s, 2)

                @pl.when(lax.rem(s, 2) == core)
                def _():
                    swap(s).wait_recv()
                    total = block(half_out, s)[...].astype(jnp.float32)
                    total = total + half_in[j].astype(jnp.float32)
                    summed[j] = total.astype(jnp.bfloat16)

                    @pl.when(j != chip)
                    def _():
                        back(j).start()

                    @pl.when(j == chip)
                    def _():
                        pltpu.make_async_copy(summed.at[j], ret_ref.at[j], l_sem.at[1]).start()

        @pl.when(i == n + lag)
        def _():
            for o in range(1, depth):
                share(o).start()

        return carry

    lax.fori_loop(0, n + 2 * lag + 1, step, 0)

    def finish(o, carry):
        j = flip(chip, o, chips)
        dispatch(j).wait_send()
        back(j).wait_send()
        home(j).wait_recv()
        return carry

    lax.fori_loop(1, chips, finish, 0)

    def finish_core(j, carry):
        forward(2 * j + core).wait_send()
        swap(2 * j + 1 - core).wait_send()
        return carry

    lax.fori_loop(0, chips, finish_core, 0)

    def finish_chain(t, carry):
        for d in range(2):
            @pl.when(places[d] < depth - 1)
            def _():
                chain(d, t).wait_send()

            @pl.when(places[d] > 0)
            def _():
                spread(d, t).wait_send()

        return carry

    lax.fori_loop(0, n, finish_chain, 0)
    for o in range(1, depth):
        share(o).wait_send()
        shared(o).wait_recv()
    own_kv.wait()
    pltpu.make_async_copy(summed.at[chip], ret_ref.at[chip], l_sem.at[1]).wait()


def expert_call(slots, features, w_gate, w_up, w_down, kv, chips, depth, cap):
    seq_len, width = features.shape
    hidden = w_gate.shape[1]
    group = 2 * chips // CHUNKS
    n = CHUNKS
    tall = group * cap
    dma = pltpu.SemaphoreType.DMA
    bf16 = jnp.bfloat16
    vmem = pl.BlockSpec(memory_space=pltpu.VMEM)
    return pl.pallas_call(
        functools.partial(expert_kernel, chips, depth, cap, group),
        out_shape=(
            jax.ShapeDtypeStruct((chips, cap, width), bf16),
            jax.ShapeDtypeStruct((depth,) + kv.shape, bf16),
        ),
        in_specs=[vmem] * 6,
        out_specs=(pl.BlockSpec(memory_space=pl.ANY), pl.BlockSpec(memory_space=pl.ANY)),
        scratch_shapes=[
            pltpu.VMEM((chips, cap, width), bf16),
            pltpu.VMEM((n, tall, width), bf16),
            pltpu.VMEM((2 * n, tall, hidden), bf16),
            pltpu.VMEM((2 * n, tall, hidden), bf16),
            pltpu.VMEM((2 * n, tall, hidden // 2), bf16),
            pltpu.VMEM((n, tall, width), bf16),
            pltpu.VMEM((chips, cap, width), bf16),
            pltpu.VMEM((chips, cap, width), bf16),
            dma((chips,)), dma((chips,)),
            dma((chips,)), dma((chips,)),
            dma((2 * n,)), dma((2 * n,)),
            dma((2 * n,)), dma((2 * n,)),
            dma((chips,)), dma((chips,)),
            dma((chips,)), dma((chips,)),
            dma((depth,)), dma((depth,)),
            dma((2,)),
        ],
        compiler_params=pltpu.CompilerParams(
            collective_id=0, has_side_effects=True, vmem_limit_bytes=58 << 20
        ),
    )(slots, features, w_gate, w_up, w_down, kv)


def attend(queries, keys, query_pos):
    query_rows = queries.shape[0]
    width = LAT + ROPE
    heads = queries.shape[1] // width
    query_heads = queries.reshape(query_rows, heads, width)
    scale = 1.0 / math.sqrt(QK_DIM)
    latents = keys[:, :LAT]
    marks = keys[:, width]
    key_pos = jnp.arange(keys.shape[0], dtype=jnp.int32)
    scores = jnp.einsum(
        "qhd,kd->hqk", query_heads, keys[:, :width], preferred_element_type=jnp.float32
    )
    scores = scores * scale
    own_key = key_pos[None, :] == query_pos[:, None]
    visible = (key_pos[None, :] <= query_pos[:, None]) & ((marks[None, :] < 0.5) | own_key)
    masked = jnp.where(visible[None], scores, -1e30)
    top = jnp.max(masked, axis=-1)
    weights = jnp.where(visible[None], jnp.exp(masked - top[:, :, None]), 0.0)
    total = jnp.sum(weights, axis=-1)
    acc = jnp.einsum(
        "hqk,kd->hqd", weights.astype(jnp.bfloat16), latents, preferred_element_type=jnp.float32
    )
    result = acc / total[:, :, None]
    result = jnp.transpose(result, (1, 0, 2)).reshape(query_rows, heads * LAT)
    return result.astype(jnp.bfloat16)


def per_device(
    hidden_in, expert_ids, route_weight, w_gate, w_up, w_down, queries, latents, rope_keys, marks
):
    features = hidden_in[0]
    seq_len = features.shape[0]
    slots_per = expert_ids.shape[2]
    chips = lax.axis_size("ep") // 2
    depth = lax.axis_size("ctx")
    capacity = max(2, 3 * seq_len * slots_per // (2 * chips))
    cap = -(-capacity // 16) * 16
    flat_ids = expert_ids[0].reshape(-1)
    onehot = (flat_ids[:, None] == jnp.arange(chips, dtype=jnp.int32)[None, :]).astype(jnp.int32)
    rank = jnp.sum(jnp.cumsum(onehot, axis=0) * onehot, axis=1) - 1
    slot = flat_ids * cap + rank
    query_rows = queries.shape[1]
    lanes = -(-(LAT + ROPE + 1) // 128) * 128
    kv = jnp.concatenate(
        [
            latents[0],
            rope_keys[0],
            jnp.broadcast_to(
                marks[0].astype(jnp.bfloat16)[:, None], (query_rows, lanes - LAT - ROPE)
            ),
        ],
        axis=1,
    )
    ret, gathered = expert_call(
        slot[None, :], features, w_gate, w_up, w_down, kv, chips, depth, cap
    )
    ret = ret.reshape(chips * cap, features.shape[1])
    pick = (slot[:, None] == jnp.arange(chips * cap, dtype=jnp.int32)[None, :]).astype(jnp.bfloat16)
    moe = jnp.dot(pick, ret, preferred_element_type=jnp.float32) * route_weight[0]
    moe = moe.astype(jnp.bfloat16)[None]
    query_pos = lax.axis_index("ctx") * query_rows + jnp.arange(query_rows, dtype=jnp.int32)
    context = attend(queries[0], gathered.reshape(-1, lanes), query_pos)[None]
    return (moe, context)


def solution(mesh):
    placed = (
        P("ep", None, "ctx"),
        P("ep", None, None),
        P("ep", None, None),
        P("ctx", "ep"),
        P("ctx", "ep"),
        P("ep", "ctx"),
        P("ep", "ctx", None),
        P("ep", "ctx", None),
        P("ep", "ctx", None),
        P("ep", "ctx"),
    )
    return jax.shard_map(
        per_device,
        mesh=mesh,
        in_specs=placed,
        out_specs=(P("ep", None, "ctx"), P("ep", "ctx", None)),
        check_vma=False,
    )
```

time: 318 us -> 148 us (0.47)
  waiting for transfers between devices: 139 us -> 0 us
  Pallas kernels: 0 us -> 119 us
  blocking collectives: 104 us -> 0 us
  local copies, waits for them, and re-layouts: 21.5 us -> 4.67 us
  between operations: 14.2 us -> 0.71 us
  matrix products: 18.5 us -> 9.99 us
  starting transfers between devices: 4.87 us -> 0 us
    psum x1 -> x0, waiting for transfers between devices: 121 us -> none  [expert_rows(): lax.psum(up_part.astype(jnp.bfloat16), 'ctx').astype(jnp.float32)]
    pallas_call x0 -> x1, Pallas kernels: none -> 119 us  [expert_call(): pl.pallas_call(functools.partial(expert_kernel, chips, depth, cap, group)...]
    all_to_all x1 -> x0, blocking collectives: 68.2 us -> none  [mixture(): lax.all_to_all(outbound, 'ep', split_axis=0, concat_axis=0, tiled=True)]
    all_gather x3 -> x0, blocking collectives: 35.9 us -> none  [the longest x1 15.2 us: attend_rows(): latent_piece = lax.all_gather(latents, 'ctx', axis=1, tiled=True)[0]]
    all_to_all x1 -> x0, waiting for transfers between devices: 18.4 us -> none  [mixture(): lax.all_to_all(produced.reshape(2 * experts, capacity, width_part), 'ep',...]
    dot_general x6 -> x3, matrix products: 18.5 us -> 9.99 us  [the longest x1 4.83 us: per_device(): jnp.dot(pick, ret, preferred_element_type=jnp.float32) * route_weight[0]]
    gather x1 -> x0, local copies, waits for them, and re-layouts: 7.7 us -> none  [mixture(): jnp.take(combined, slot, axis=0).reshape(seq_len, slots_per, width_part)]
    convert_element_type x4 -> x2, other arithmetic: 8.03 us -> 1.34 us  [the longest x1 0.69 us: per_device(): (flat_ids[:, None] == jnp.arange(chips, dtype=jnp.int32)[None, :]).astype...]
  transfers between devices with their start and end apart: 2 -> 0, of which waited for: 2 -> 0; matrix products, arithmetic and copies ran while one was open for 3% -> 0% of each run, Pallas kernels for 0% -> 0%
where the time goes in v1:
time: 148 us; the launch traced here: 147 us
  Pallas kernels  119 us (80%)
  other arithmetic  13 us (9%)
  matrix products  9.99 us (7%)
  local copies, waits for them, and re-layouts  4.67 us (3%)
    pallas_call x1, Pallas kernels, expert_call(): pl.pallas_call(functools.partial(expert_kernel, chips, depth, cap, group)...  119 us
    dot_general x1, matrix products, per_device(): jnp.dot(pick, ret, preferred_element_type=jnp.float32) * route_weight[0]  4.83 us
    sub x1, other arithmetic, attend(): weights = jnp.where(visible[None], jnp.exp(masked - top[:, :, None]), 0.0)  4.6 us
    dot_general x1, matrix products, attend(): jnp.einsum('qhd,kd->hqk', query_heads, keys[:, :width], preferred_element...  4.14 us
    unnamed x9, local copies, waits for them, and re-layouts  3.48 us

profile of v1, /device:TPU:0, one launch (start us, length us, event | category | flops | bytes accessed | tf_op | source)
XLA Modules:
  0.0 147.4 jit_solution(8192596861895280003)
XLA Ops:
  0.6 0.7 fusion.14
  1.3 1.2 reduce-window.6
  2.5 0.2 slice_reduce_fusion
  2.7 0.2 reduce-window.9
  2.9 0.1 add_bitcast_fusion
  3.0 0.7 fusion.13
  3.7 0.7 multiply_add_fusion
  4.4 1.3 bitcast_add_fusion.slot_ref
  5.7 0.7 convert_bitcast_fusion
  6.3 0.1 broadcast_in_dim.22
  6.4 0.8 copy.16
  7.2 1.7 %pad_maximum_fusion.kv_ref = bf16[128,640]{1,0:T(8,128)(2,1)} fusion(bf16[128,64]{1,0:T(8,128)(2,1)S(1)} %broadcast_in_dim.22, bf16[128,64]{1,0:T(8,128)(2,1)S(1)} %bitcast.62, bf16[128,512]{1,0:T(8,128)(2,1)} %bitcast.61), kind=kLoop, calls=%fused_computation.22 | loop fusion | flops 491520 | bytes 327680 | tf_op jit(solution)/shard_map/concatenate | solution.py:415
  8.9 0.0 copy-start.2
  8.9 119.0 %shard_map.113 = (bf16[4,192,1792]{2,1,0:T(8,128)(2,1)}, bf16[4,128,640]{2,1,0:T(8,128)(2,1)}) custom-call(s32[1,512]{1,0:T(1,128)} %bitcast_add_fusion.slot_ref, bf16[512,1792]{1,0:T(8,128)(2,1)} %bitcast.59, bf16[1792,512]{1,0:T(8,128)(2,1)} %gate_ref.1, bf16[1792,512]{1,0:T(8,128)(2,1)} %up_ref.1, bf16[512,1792]{1,0:T(8,128)(2,1)} %down_ref.1, ...), custom_call_target="tpu_custom_call" | custom-call | tf_op jit(solution)/shard_map/pallas_call | solution.py:340
  127.9 0.0 copy-done.2
  127.9 0.0 copy-start
  127.9 4.8 %fusion.2 = bf16[1,512,1792]{2,1,0:T(8,128)(2,1)} fusion(bf16[768,1792]{1,0:T(8,128)(2,1)} %bitcast.71, f32[512]{0:T(512)S(1)} %bitcast.72, s32[512]{0:T(512)S(1)} %get-tuple-element.8), kind=kOutput, calls=%fused_computation.6 | convolution fusion | flops 1411514368 | bytes 4591616 | tf_op jit(solution)/shard_map/dot_general | solution.py:430
  132.8 0.0 copy-done
  132.8 1.1 copy.18
  133.8 4.1 %fusion.9 = f32[512,128,12]{1,0,2:T(8,128)} fusion(bf16[128,12,576]{0,2,1:T(8,128)(2,1)S(1)} %bitcast.60, bf16[512,640]{1,0:T(8,128)(2,1)} %bitcast.66), kind=kOutput, calls=%fused_computation.15 | convolution fusion | flops 905969664 | bytes 5570560 | tf_op jit(solution)/shard_map/qhd,kd->hqk/dot_general | solution.py:381
  138.0 1.1 compare_reduce_fusion
  139.1 0.1 fusion.10
  139.3 0.0 copy-start.1
  139.3 4.6 %fusion.17 = (f32[12,128]{1,0:T(8,128)S(1)}, bf16[12,128,512]{1,2,0:T(8,128)(2,1)S(1)}) fusion(f32[512,128,12]{1,0,2:T(8,128)} %fusion.9, pred[128,512]{0,1:T(8,128)(4,1)S(1)} %fusion.10), kind=kOutput, calls=%fused_computation.38 | output fusion | flops 6291967 | bytes 4790272 | tf_op jit(solution)/shard_map/sub | solution.py:389
  143.9 0.0 copy-done.1
  143.9 1.0 fusion.1
  144.9 0.9 copy.20
  145.8 1.6 %copy.21 = bf16[1,128,6144]{2,1,0:T(8,128)(2,1)} copy(bf16[1,128,6144]{1,2,0:T(8,128)(2,1)S(1)} %bitcast.58) | data formatting | bytes 3145728
  (1 shorter events, 0.0 us)
Async XLA Ops:
  8.9 119.0 %copy-start.2 = (f32[1,512,1]{1,2,0:T(1,128)S(1)}, f32[1,512,1]{1,2,0:T(1,128)}, u32[]{:S(2)}) copy-start(f32[1,512,1]{1,2,0:T(1,128)} %param.12) | copy-start | bytes 6148
  127.9 4.8 %copy-start = (bf16[1,128,6912]{2,1,0:T(8,128)(2,1)S(1)}, bf16[1,128,6912]{2,1,0:T(8,128)(2,1)}, u32[]{:S(2)}) copy-start(bf16[1,128,6912]{2,1,0:T(8,128)(2,1)} %param.16) | copy-start | bytes 5308420
  139.3 4.6 %copy-start.1 = (bf16[4,128,640]{2,1,0:T(8,128)(2,1)S(1)}, bf16[4,128,640]{2,1,0:T(8,128)(2,1)}, u32[]{:S(2)}) copy-start(bf16[4,128,640]{2,1,0:T(8,128)(2,1)} %get-tuple-element.5) | copy-start | bytes 1966084

commit v2 on v1

--- a/solution.py
+++ b/solution.py
@@ -29,14 +29,22 @@
     depth,
     cap,
     group,
-    slot_ref,
+    ids_ref,
     feat_ref,
+    weight_ref,
     gate_ref,
     up_ref,
     down_ref,
-    kv_ref,
+    query_ref,
+    lat_ref,
+    rope_ref,
+    mark_ref,
+    moe_ref,
+    ctx_ref,
+    gat_ref,
     ret_ref,
-    gat_ref,
+    keys_ref,
+    seen_ref,
     packed,
     rows,
     part_out,
@@ -59,7 +67,6 @@
     r_recv,
     g_send,
     g_recv,
-    l_sem,
 ):
     me = lax.axis_index("ep")
     z = lax.axis_index("ctx")
@@ -118,11 +125,11 @@
 
     def share(o):
         other = lax.rem(z + o, depth)
-        return remote(kv_ref, gat_ref.at[z], g_send.at[o], g_recv.at[o], ctx=other)
+        return remote(gat_ref.at[z], gat_ref.at[z], g_send.at[o], g_recv.at[o], ctx=other)
 
     def shared(o):
         other = lax.rem(z + depth - o, depth)
-        return remote(kv_ref, gat_ref.at[other], g_send.at[o], g_recv.at[o], ctx=other)
+        return remote(gat_ref.at[z], gat_ref.at[other], g_send.at[o], g_recv.at[o], ctx=other)
 
     barrier = pltpu.get_barrier_semaphore()
 
@@ -138,13 +145,34 @@
         pl.semaphore_signal(
             barrier, inc=1, device_id={"ctx": lax.rem(z + o, depth)}, device_id_type=MESH
         )
+
+    bf16, f32 = jnp.bfloat16, jnp.float32
+    iota = lax.broadcasted_iota
+    query_rows = query_ref.shape[0]
+    lanes = gat_ref.shape[2]
+    width_k = LAT + ROPE
+    eye = iota(jnp.int32, (query_rows, query_rows), 0) == iota(jnp.int32, (query_rows, query_rows), 1)
+    mark_col = jnp.sum(jnp.where(eye, mark_ref[...].astype(f32), 0.0), axis=1, keepdims=True)
+    gat_ref[z, :, :LAT] = lat_ref[...]
+    gat_ref[z, :, LAT:width_k] = rope_ref[...]
+    gat_ref[z, :, width_k:] = jnp.broadcast_to(mark_col, (query_rows, lanes - width_k)).astype(bf16)
+
+    ids = ids_ref[...]
+    tokens = ids.shape[1]
+    kinds = max(chips, 16)
+    named = iota(jnp.int32, (kinds, tokens), 0) == ids
+    earlier = iota(jnp.int32, (tokens, tokens), 0) < iota(jnp.int32, (tokens, tokens), 1)
+    counts = jnp.dot(
+        jnp.where(named, 1.0, 0.0).astype(bf16),
+        jnp.where(earlier, 1.0, 0.0).astype(bf16),
+        preferred_element_type=f32,
+    )
+    rank = jnp.sum(jnp.where(named, counts, 0.0), axis=0, keepdims=True)
+    slots = ids * cap + rank.astype(jnp.int32)
+
     pl.semaphore_wait(barrier, chips + depth - 1)
-
-    own_kv = pltpu.make_async_copy(kv_ref, gat_ref.at[z], l_sem.at[0])
-    own_kv.start()
-
-    slots = slot_ref[...]
-    tokens = slots.shape[1]
+    for o in range(1, depth):
+        share(o).start()
 
     def pack(o, carry):
         j = flip(chip, o, chips)
@@ -153,10 +181,7 @@
         chosen = jnp.dot(pick, feat_ref[...], preferred_element_type=jnp.float32)
         packed[j] = chosen.astype(jnp.bfloat16)
 
-        @pl.when(o < chips)
-        def _():
-            dispatch(j).start()
-
+        dispatch(j).start()
         return carry
 
     lax.fori_loop(1, chips, pack, 0)
@@ -168,7 +193,56 @@
     first = lax.div(me, group)
     lag = depth - 1
 
+    heads = query_ref.shape[1] // width_k
+    scale = 1.0 / math.sqrt(QK_DIM)
+
+    def prepare():
+        for o in range(1, depth):
+            shared(o).wait_recv()
+        count = depth * query_rows
+        keys = gat_ref[...].reshape(count, lanes)
+        row = iota(jnp.int32, (lanes, lanes), 0)
+        column = iota(jnp.int32, (lanes, lanes), 1)
+        even = (row == column) & (row < width_k)
+        odd = row == column + (lanes - width_k)
+        contract = (((1,), (1,)), ((), ()))
+        for a, chosen in ((0, even), (1, odd)):
+            pick = jnp.where(chosen, 1.0, 0.0).astype(bf16)
+            keys_ref[a] = lax.dot_general(
+                pick, keys, contract, preferred_element_type=f32
+            ).astype(bf16)
+        pick = jnp.where(iota(jnp.int32, (16, lanes), 1) == width_k, 1.0, 0.0).astype(bf16)
+        marks = lax.dot_general(pick, keys, contract, preferred_element_type=f32)[:1]
+        query_pos = z * query_rows + iota(jnp.int32, (query_rows, count), 0)
+        key_pos = iota(jnp.int32, (query_rows, count), 1)
+        visible = (key_pos == query_pos) | ((key_pos < query_pos) & (marks < 0.5))
+        seen_ref[...] = jnp.where(visible, 0.0, -1e30)
+
+    def attend_pair(pair):
+        latents = gat_ref[:, :, :LAT].reshape(depth * query_rows, LAT)
+        base = pl.multiple_of(pair * (2 * width_k), 128)
+        mask = seen_ref[...]
+        for a in range(2):
+            shift = a * (2 * width_k - lanes)
+            q = query_ref[:, pl.ds(pl.multiple_of(base + shift, 128), lanes)]
+            scores = jnp.dot(q, keys_ref[a], preferred_element_type=f32) * scale
+            masked = jnp.where(mask < 0.0, -1e30, scores)
+            top = jnp.max(masked, axis=1, keepdims=True)
+            weight = jnp.where(mask < 0.0, 0.0, jnp.exp(masked - top))
+            total = jnp.sum(weight, axis=1, keepdims=True)
+            acc = jnp.dot(weight.astype(bf16), latents, preferred_element_type=f32)
+            where = pl.multiple_of((2 * pair + a) * LAT, 128)
+            ctx_ref[:, pl.ds(where, LAT)] = (acc / total).astype(bf16)
+
     def step(i, carry):
+        @pl.when(i == 1)
+        def _():
+            prepare()
+
+        @pl.when((i >= 2) & (i < 2 + heads // 2))
+        def _():
+            attend_pair(i - 2)
+
         @pl.when(i < n)
         def _():
             q = flip(first, i, n)
@@ -281,22 +355,33 @@
 
                     @pl.when(j == chip)
                     def _():
-                        pltpu.make_async_copy(summed.at[j], ret_ref.at[j], l_sem.at[1]).start()
-
-        @pl.when(i == n + lag)
-        def _():
-            for o in range(1, depth):
-                share(o).start()
-
-        return carry
-
-    lax.fori_loop(0, n + 2 * lag + 1, step, 0)
+                        ret_ref[j] = total.astype(jnp.bfloat16)
+
+        return carry
+
+    lax.fori_loop(0, max(n + 2 * lag + 1, 2 + heads // 2), step, 0)
+
+    def land(o, carry):
+        home(flip(chip, o, chips)).wait_recv()
+        return carry
+
+    lax.fori_loop(1, chips, land, 0)
+    diagonal = iota(jnp.int32, (tokens, tokens), 0) == iota(jnp.int32, (tokens, tokens), 1)
+    slot_col = jnp.sum(jnp.where(diagonal, slots, 0), axis=1, keepdims=True)
+    pick = jnp.where(iota(jnp.int32, (tokens, chips * cap), 1) == slot_col, 1.0, 0.0).astype(bf16)
+    tile = 256
+    for w in range(0, width, tile):
+        mixed = jnp.dot(
+            pick,
+            ret_ref[:, :, w:w + tile].reshape(chips * cap, tile),
+            preferred_element_type=f32,
+        )
+        moe_ref[:, w:w + tile] = (mixed * weight_ref[...]).astype(bf16)
 
     def finish(o, carry):
         j = flip(chip, o, chips)
         dispatch(j).wait_send()
         back(j).wait_send()
-        home(j).wait_recv()
         return carry
 
     lax.fori_loop(1, chips, finish, 0)
@@ -323,29 +408,33 @@
     lax.fori_loop(0, n, finish_chain, 0)
     for o in range(1, depth):
         share(o).wait_send()
-        shared(o).wait_recv()
-    own_kv.wait()
-    pltpu.make_async_copy(summed.at[chip], ret_ref.at[chip], l_sem.at[1]).wait()
-
-
-def expert_call(slots, features, w_gate, w_up, w_down, kv, chips, depth, cap):
+
+
+def expert_call(ids, features, weight, w_gate, w_up, w_down, queries, latents, ropes, marks, chips, depth, cap):
     seq_len, width = features.shape
     hidden = w_gate.shape[1]
     group = 2 * chips // CHUNKS
     n = CHUNKS
     tall = group * cap
+    query_rows = queries.shape[0]
+    heads = queries.shape[1] // (LAT + ROPE)
+    lanes = -(-(LAT + ROPE + 1) // 128) * 128
     dma = pltpu.SemaphoreType.DMA
     bf16 = jnp.bfloat16
     vmem = pl.BlockSpec(memory_space=pltpu.VMEM)
     return pl.pallas_call(
         functools.partial(expert_kernel, chips, depth, cap, group),
         out_shape=(
-            jax.ShapeDtypeStruct((chips, cap, width), bf16),
-            jax.ShapeDtypeStruct((depth,) + kv.shape, bf16),
+            jax.ShapeDtypeStruct((seq_len, width), bf16),
+            jax.ShapeDtypeStruct((query_rows, heads * LAT), bf16),
         ),
-        in_specs=[vmem] * 6,
-        out_specs=(pl.BlockSpec(memory_space=pl.ANY), pl.BlockSpec(memory_space=pl.ANY)),
+        in_specs=[vmem] * 10,
+        out_specs=(vmem, vmem),
         scratch_shapes=[
+            pltpu.VMEM((depth, query_rows, lanes), bf16),
+            pltpu.VMEM((chips, cap, width), bf16),
+            pltpu.VMEM((2, lanes, depth * query_rows), bf16),
+            pltpu.VMEM((query_rows, depth * query_rows), jnp.float32),
             pltpu.VMEM((chips, cap, width), bf16),
             pltpu.VMEM((n, tall, width), bf16),
             pltpu.VMEM((2 * n, tall, hidden), bf16),
@@ -361,39 +450,11 @@
             dma((chips,)), dma((chips,)),
             dma((chips,)), dma((chips,)),
             dma((depth,)), dma((depth,)),
-            dma((2,)),
         ],
         compiler_params=pltpu.CompilerParams(
-            collective_id=0, has_side_effects=True, vmem_limit_bytes=58 << 20
+            collective_id=0, has_side_effects=True, vmem_limit_bytes=60 << 20
         ),
-    )(slots, features, w_gate, w_up, w_down, kv)
-
-
-def attend(queries, keys, query_pos):
-    query_rows = queries.shape[0]
-    width = LAT + ROPE
-    heads = queries.shape[1] // width
-    query_heads = queries.reshape(query_rows, heads, width)
-    scale = 1.0 / math.sqrt(QK_DIM)
-    latents = keys[:, :LAT]
-    marks = keys[:, width]
-    key_pos = jnp.arange(keys.shape[0], dtype=jnp.int32)
-    scores = jnp.einsum(
-        "qhd,kd->hqk", query_heads, keys[:, :width], preferred_element_type=jnp.float32
-    )
-    scores = scores * scale
-    own_key = key_pos[None, :] == query_pos[:, None]
-    visible = (key_pos[None, :] <= query_pos[:, None]) & ((marks[None, :] < 0.5) | own_key)
-    masked = jnp.where(visible[None], scores, -1e30)
-    top = jnp.max(masked, axis=-1)
-    weights = jnp.where(visible[None], jnp.exp(masked - top[:, :, None]), 0.0)
-    total = jnp.sum(weights, axis=-1)
-    acc = jnp.einsum(
-        "hqk,kd->hqd", weights.astype(jnp.bfloat16), latents, preferred_element_type=jnp.float32
-    )
-    result = acc / total[:, :, None]
-    result = jnp.transpose(result, (1, 0, 2)).reshape(query_rows, heads * LAT)
-    return result.astype(jnp.bfloat16)
+    )(ids, features, weight, w_gate, w_up, w_down, queries, latents, ropes, marks)
 
 
 def per_device(
@@ -406,32 +467,22 @@
     depth = lax.axis_size("ctx")
     capacity = max(2, 3 * seq_len * slots_per // (2 * chips))
     cap = -(-capacity // 16) * 16
-    flat_ids = expert_ids[0].reshape(-1)
-    onehot = (flat_ids[:, None] == jnp.arange(chips, dtype=jnp.int32)[None, :]).astype(jnp.int32)
-    rank = jnp.sum(jnp.cumsum(onehot, axis=0) * onehot, axis=1) - 1
-    slot = flat_ids * cap + rank
-    query_rows = queries.shape[1]
-    lanes = -(-(LAT + ROPE + 1) // 128) * 128
-    kv = jnp.concatenate(
-        [
-            latents[0],
-            rope_keys[0],
-            jnp.broadcast_to(
-                marks[0].astype(jnp.bfloat16)[:, None], (query_rows, lanes - LAT - ROPE)
-            ),
-        ],
-        axis=1,
+    moe, context = expert_call(
+        expert_ids[0].reshape(1, -1),
+        features,
+        route_weight[0],
+        w_gate,
+        w_up,
+        w_down,
+        queries[0],
+        latents[0],
+        rope_keys[0],
+        marks,
+        chips,
+        depth,
+        cap,
     )
-    ret, gathered = expert_call(
-        slot[None, :], features, w_gate, w_up, w_down, kv, chips, depth, cap
-    )
-    ret = ret.reshape(chips * cap, features.shape[1])
-    pick = (slot[:, None] == jnp.arange(chips * cap, dtype=jnp.int32)[None, :]).astype(jnp.bfloat16)
-    moe = jnp.dot(pick, ret, preferred_element_type=jnp.float32) * route_weight[0]
-    moe = moe.astype(jnp.bfloat16)[None]
-    query_pos = lax.axis_index("ctx") * query_rows + jnp.arange(query_rows, dtype=jnp.int32)
-    context = attend(queries[0], gathered.reshape(-1, lanes), query_pos)[None]
-    return (moe, context)
+    return (moe[None], context[None])
 
 
 def solution(mesh):

time: 148 us -> 134 us (0.905)
  other arithmetic: 13 us -> 0 us
  matrix products: 9.99 us -> 0 us
  Pallas kernels: 119 us -> 126 us
  local copies, waits for them, and re-layouts: 4.67 us -> 7.08 us
    dot_general x3 -> x0, matrix products: 9.99 us -> none  [the longest x1 4.83 us: per_device(): jnp.dot(pick, ret, preferred_element_type=jnp.float32) * route_weight[0]]
    pallas_call x1, Pallas kernels: 119 us -> 126 us  [expert_call(): pl.pallas_call(functools.partial(expert_kernel, chips, depth, cap, group)...]
    sub x1 -> x0, other arithmetic: 4.6 us -> none  [attend(): weights = jnp.where(visible[None], jnp.exp(masked - top[:, :, None]), 0.0)]
    unnamed x9 -> x5, local copies, waits for them, and re-layouts: 3.48 us -> 5.54 us
    add x3 -> x0, other arithmetic: 1.95 us -> none  [the longest x2 1.95 us: per_device(): slot = flat_ids * cap + rank]
    concatenate x1 -> x0, other arithmetic: 1.67 us -> none  [per_device(): jnp.concatenate([latents[0], rope_keys[0], jnp.broadcast_to(marks[0].asty...]
    squeeze x0 -> x1, local copies, waits for them, and re-layouts: none -> 1.53 us  [per_device(): route_weight[0]]
where the time goes in v2:
time: 134 us
  Pallas kernels  126 us (94%)
  local copies, waits for them, and re-layouts  7.08 us (5%)
    pallas_call x1, Pallas kernels, expert_call(): pl.pallas_call(functools.partial(expert_kernel, chips, depth, cap, group)...  126 us
    unnamed x5, local copies, waits for them, and re-layouts  5.54 us

profile of v2, /device:TPU:0, one launch (start us, length us, event | category | flops | bytes accessed | tf_op | source)
XLA Modules:
  0.0 133.6 jit_solution(811506734517980550)
XLA Ops:
  0.6 1.4 %copy.13 = bf16[1,128,64]{2,1,0:T(8,128)(2,1)} copy(bf16[1,128,64]{1,2,0:T(8,128)(2,1)} %param.18) | data formatting | bytes 32768 | tf_op args[8]
  2.1 1.5 %copy.14.weight_ref = f32[512,1]{1,0:T(8,128)} copy(f32[512,1]{0,1:T(1,128)} %bitcast.14) | data formatting | bytes 4096 | tf_op jit(solution)/shard_map/squeeze | solution.py:473
  3.6 125.9 %shard_map.113 = (bf16[512,1792]{1,0:T(8,128)(2,1)}, bf16[128,6144]{1,0:T(8,128)(2,1)}) custom-call(s32[1,512]{1,0:T(1,128)} %bitcast.15, bf16[512,1792]{1,0:T(8,128)(2,1)} %bitcast.9, f32[512,1]{1,0:T(8,128)} %copy.14.weight_ref, bf16[1792,512]{1,0:T(8,128)(2,1)} %gate_ref.1, bf16[1792,512]{1,0:T(8,128)(2,1)} %up_ref.1, bf16[512,1792]{1,0:T(8,128)(2,1)} %down_ref.1, ...), custom_call_target="tpu_custom_call" | custom-call | tf_op jit(solution)/shard_map/pallas_call | solution.py:425
  129.5 0.0 copy-start
  129.5 3.0 %copy.17 = bf16[1,512,1792]{2,1,0:T(8,128)(2,1)} copy(bf16[1,512,1792]{2,1,0:T(8,128)(2,1)} %bitcast.8) | data formatting | bytes 3670016
  132.5 0.0 copy-done
  132.5 1.1 copy.18
Async XLA Ops:
  129.5 3.0 %copy-start = (bf16[128,6144]{1,0:T(8,128)(2,1)S(1)}, bf16[128,6144]{1,0:T(8,128)(2,1)}, u32[]{:S(2)}) copy-start(bf16[128,6144]{1,0:T(8,128)(2,1)} %get-tuple-element.5) | copy-start | bytes 4718596

commit v3 on v2

--- a/solution.py
+++ b/solution.py
@@ -11,7 +11,9 @@
 LAT = 512
 ROPE = 64
 QK_DIM = 192
-CHUNKS = 8
+CHUNKS = 16
+FAR = 4
+LAG = 2
 MESH = pl.DeviceIdType.MESH
 
 
@@ -28,6 +30,7 @@
     chips,
     depth,
     cap,
+    split,
     group,
     ids_ref,
     feat_ref,
@@ -77,13 +80,19 @@
     hidden = gate_ref.shape[1]
     quarter = hidden // 2
     n = CHUNKS
-    block_rows = group * cap
-
-    def block(buf, source):
+    unit = cap // split
+
+    def block(buf, v):
         if group == 1:
-            return buf.at[source]
-        start = pl.multiple_of(lax.rem(source, group) * cap, cap)
-        return buf.at[lax.div(source, group), pl.ds(start, cap)]
+            return buf.at[v]
+        start = pl.multiple_of(lax.rem(v, group) * unit, unit)
+        return buf.at[lax.div(v, group), pl.ds(start, unit)]
+
+    def pair_of(v):
+        return lax.div(v, 2 * split) * split + lax.rem(v, split)
+
+    def core_of(v):
+        return lax.rem(lax.div(v, split), 2)
 
     def remote(src, dst, send, recv, **device):
         return pltpu.make_async_remote_copy(
@@ -91,15 +100,22 @@
             device_id=device, device_id_type=MESH,
         )
 
-    def dispatch(j):
-        return remote(packed.at[j], block(rows, me), d_send.at[j], d_recv.at[chip], ep=2 * j + core)
-
-    def arrival(j):
-        return remote(packed.at[j], block(rows, 2 * j + core), d_send.at[j], d_recv.at[j], ep=2 * j + core)
-
-    def forward(s):
-        j = lax.div(s, 2)
-        return remote(block(rows, s), block(rows, s), f_send.at[j], f_recv.at[j], ep=sibling)
+    def peer(m):
+        return 2 * lax.div(m, split) + core
+
+    def dispatch(m):
+        h = lax.rem(m, split)
+        return remote(
+            packed.at[m], block(rows, me * split + h), d_send.at[m], d_recv.at[chip * split + h], ep=peer(m)
+        )
+
+    def arrival(m):
+        v = peer(m) * split + lax.rem(m, split)
+        return remote(packed.at[m], block(rows, v), d_send.at[m], d_recv.at[m], ep=peer(m))
+
+    def forward(v):
+        m = pair_of(v)
+        return remote(block(rows, v), block(rows, v), f_send.at[m], f_recv.at[m], ep=sibling)
 
     nexts = (z + 1, z - 1)
     prevs = (z - 1, z + 1)
@@ -113,15 +129,18 @@
         at = d * n + t
         return remote(hid.at[at], hid.at[at], b_send.at[at], b_recv.at[at], ctx=prevs[d])
 
-    def swap(s):
-        j = lax.div(s, 2)
-        return remote(block(half_out, s), half_in.at[j], h_send.at[j], h_recv.at[j], ep=sibling)
-
-    def back(j):
-        return remote(summed.at[j], ret_ref.at[chip], r_send.at[j], r_recv.at[chip], ep=2 * j + core)
-
-    def home(j):
-        return remote(summed.at[j], ret_ref.at[j], r_send.at[j], r_recv.at[j], ep=2 * j + core)
+    def swap(v):
+        m = pair_of(v)
+        return remote(block(half_out, v), half_in.at[m], h_send.at[m], h_recv.at[m], ep=sibling)
+
+    def back(m):
+        h = lax.rem(m, split)
+        return remote(
+            summed.at[m], ret_ref.at[chip * split + h], r_send.at[m], r_recv.at[chip * split + h], ep=peer(m)
+        )
+
+    def home(m):
+        return remote(summed.at[m], ret_ref.at[m], r_send.at[m], r_recv.at[m], ep=peer(m))
 
     def share(o):
         other = lax.rem(z + o, depth)
@@ -153,6 +172,11 @@
     width_k = LAT + ROPE
     eye = iota(jnp.int32, (query_rows, query_rows), 0) == iota(jnp.int32, (query_rows, query_rows), 1)
     mark_col = jnp.sum(jnp.where(eye, mark_ref[...].astype(f32), 0.0), axis=1, keepdims=True)
+    for o in range(1, depth):
+        @pl.when(o > z)
+        def _():
+            gat_ref[o] = jnp.zeros((query_rows, lanes), bf16)
+
     gat_ref[z, :, :LAT] = lat_ref[...]
     gat_ref[z, :, LAT:width_k] = rope_ref[...]
     gat_ref[z, :, width_k:] = jnp.broadcast_to(mark_col, (query_rows, lanes - width_k)).astype(bf16)
@@ -172,33 +196,44 @@
 
     pl.semaphore_wait(barrier, chips + depth - 1)
     for o in range(1, depth):
-        share(o).start()
+        @pl.when(z + o < depth)
+        def _():
+            share(o).start()
 
     def pack(o, carry):
         j = flip(chip, o, chips)
         index = j * cap + lax.broadcasted_iota(jnp.int32, (cap, tokens), 0)
         pick = jnp.where(index == slots, 1.0, 0.0).astype(jnp.bfloat16)
         chosen = jnp.dot(pick, feat_ref[...], preferred_element_type=jnp.float32)
-        packed[j] = chosen.astype(jnp.bfloat16)
-
-        dispatch(j).start()
+        for h in range(split):
+            packed[j * split + h] = chosen[h * unit:(h + 1) * unit].astype(bf16)
+
+        @pl.when(o < 3)
+        def _():
+            for h in range(split):
+                dispatch(j * split + h).start()
+
         return carry
 
     lax.fori_loop(1, chips, pack, 0)
     index = chip * cap + lax.broadcasted_iota(jnp.int32, (cap, tokens), 0)
     pick = jnp.where(index == slots, 1.0, 0.0).astype(jnp.bfloat16)
     chosen = jnp.dot(pick, feat_ref[...], preferred_element_type=jnp.float32)
-    block(rows, me)[...] = chosen.astype(jnp.bfloat16)
-
-    first = lax.div(me, group)
-    lag = depth - 1
+    for h in range(split):
+        block(rows, me * split + h)[...] = chosen[h * unit:(h + 1) * unit].astype(bf16)
+
+    first = lax.div(me * split, group)
+    lag = LAG * (depth - 1)
 
     heads = query_ref.shape[1] // width_k
     scale = 1.0 / math.sqrt(QK_DIM)
 
     def prepare():
         for o in range(1, depth):
-            shared(o).wait_recv()
+            @pl.when(z >= o)
+            def _():
+                shared(o).wait_recv()
+
         count = depth * query_rows
         keys = gat_ref[...].reshape(count, lanes)
         row = iota(jnp.int32, (lanes, lanes), 0)
@@ -243,31 +278,40 @@
         def _():
             attend_pair(i - 2)
 
+        @pl.when(i == (FAR if chips == 4 else 0))
+        def _():
+            def far(o, carry):
+                j = flip(chip, o, chips)
+                for h in range(split):
+                    dispatch(j * split + h).start()
+                return carry
+
+            lax.fori_loop(3, chips, far, 0)
+
         @pl.when(i < n)
         def _():
             q = flip(first, i, n)
             for g in range(group):
-                s = q * group + g
-                j = lax.div(s, 2)
-                mine = lax.rem(s, 2) == core
-
-                @pl.when(mine & (j != chip))
-                def _():
-                    arrival(j).wait_recv()
+                v = q * group + g
+                mine = core_of(v) == core
+
+                @pl.when(mine & (lax.div(v, 2 * split) != chip))
+                def _():
+                    arrival(pair_of(v)).wait_recv()
 
                 @pl.when(mine)
                 def _():
-                    forward(s).start()
+                    forward(v).start()
 
             for g in range(group):
-                s = q * group + g
-
-                @pl.when(lax.rem(s, 2) != core)
-                def _():
-                    forward(s).wait_recv()
+                v = q * group + g
+
+                @pl.when(core_of(v) != core)
+                def _():
+                    forward(v).wait_recv()
 
         for d in range(2):
-            t = i - places[d]
+            t = i - LAG * places[d]
             lo, hi = d * quarter, (d + 1) * quarter
 
             @pl.when((t >= 0) & (t < n))
@@ -302,7 +346,7 @@
                         spread(d, t).start()
 
         for d in range(2):
-            t = i - lag - (depth - 1 - places[d])
+            t = i - lag - LAG * (depth - 1 - places[d])
 
             @pl.when((t >= 0) & (t < n) & (places[d] < depth - 1))
             def _():
@@ -327,47 +371,49 @@
                 )
                 half_out[q, :, w:w + tile] = got.astype(jnp.bfloat16)
             for g in range(group):
-                s = q * group + g
-
-                @pl.when(lax.rem(s, 2) != core)
-                def _():
-                    swap(s).start()
-
-        t2 = i - 2 * lag - 1
+                v = q * group + g
+
+                @pl.when(core_of(v) != core)
+                def _():
+                    swap(v).start()
+
+        t2 = i - 2 * lag - split
 
         @pl.when((t2 >= 0) & (t2 < n))
         def _():
             q = flip(first, t2, n)
             for g in range(group):
-                s = q * group + g
-                j = lax.div(s, 2)
-
-                @pl.when(lax.rem(s, 2) == core)
-                def _():
-                    swap(s).wait_recv()
-                    total = block(half_out, s)[...].astype(jnp.float32)
-                    total = total + half_in[j].astype(jnp.float32)
-                    summed[j] = total.astype(jnp.bfloat16)
-
-                    @pl.when(j != chip)
+                v = q * group + g
+                m = pair_of(v)
+                local = lax.div(m, split) == chip
+
+                @pl.when(core_of(v) == core)
+                def _():
+                    swap(v).wait_recv()
+                    total = block(half_out, v)[...].astype(f32) + half_in[m].astype(f32)
+                    summed[m] = total.astype(bf16)
+
+                    @pl.when(jnp.logical_not(local))
                     def _():
-                        back(j).start()
-
-                    @pl.when(j == chip)
+                        back(m).start()
+
+                    @pl.when(local)
                     def _():
-                        ret_ref[j] = total.astype(jnp.bfloat16)
-
-        return carry
-
-    lax.fori_loop(0, max(n + 2 * lag + 1, 2 + heads // 2), step, 0)
+                        ret_ref[m] = total.astype(bf16)
+
+        return carry
+
+    lax.fori_loop(0, max(n + 2 * lag + split, 2 + heads // 2), step, 0)
 
     def land(o, carry):
-        home(flip(chip, o, chips)).wait_recv()
+        for h in range(split):
+            home(flip(chip, o, chips) * split + h).wait_recv()
         return carry
 
     lax.fori_loop(1, chips, land, 0)
     diagonal = iota(jnp.int32, (tokens, tokens), 0) == iota(jnp.int32, (tokens, tokens), 1)
     slot_col = jnp.sum(jnp.where(diagonal, slots, 0), axis=1, keepdims=True)
+    weight_col = jnp.sum(jnp.where(diagonal, weight_ref[...], 0.0), axis=1, keepdims=True)
     pick = jnp.where(iota(jnp.int32, (tokens, chips * cap), 1) == slot_col, 1.0, 0.0).astype(bf16)
     tile = 256
     for w in range(0, width, tile):
@@ -376,19 +422,21 @@
             ret_ref[:, :, w:w + tile].reshape(chips * cap, tile),
             preferred_element_type=f32,
         )
-        moe_ref[:, w:w + tile] = (mixed * weight_ref[...]).astype(bf16)
+        moe_ref[:, w:w + tile] = (mixed * weight_col).astype(bf16)
 
     def finish(o, carry):
         j = flip(chip, o, chips)
-        dispatch(j).wait_send()
-        back(j).wait_send()
+        for h in range(split):
+            dispatch(j * split + h).wait_send()
+            back(j * split + h).wait_send()
         return carry
 
     lax.fori_loop(1, chips, finish, 0)
 
     def finish_core(j, carry):
-        forward(2 * j + core).wait_send()
-        swap(2 * j + 1 - core).wait_send()
+        for h in range(split):
+            forward((2 * j + core) * split + h).wait_send()
+            swap((2 * j + 1 - core) * split + h).wait_send()
         return carry
 
     lax.fori_loop(0, chips, finish_core, 0)
@@ -407,15 +455,20 @@
 
     lax.fori_loop(0, n, finish_chain, 0)
     for o in range(1, depth):
-        share(o).wait_send()
+        @pl.when(z + o < depth)
+        def _():
+            share(o).wait_send()
 
 
 def expert_call(ids, features, weight, w_gate, w_up, w_down, queries, latents, ropes, marks, chips, depth, cap):
     seq_len, width = features.shape
     hidden = w_gate.shape[1]
-    group = 2 * chips // CHUNKS
+    split = max(1, CHUNKS // (2 * chips))
+    group = 2 * chips * split // CHUNKS
     n = CHUNKS
-    tall = group * cap
+    unit = cap // split
+    tall = group * unit
+    pairs = chips * split
     query_rows = queries.shape[0]
     heads = queries.shape[1] // (LAT + ROPE)
     lanes = -(-(LAT + ROPE + 1) // 128) * 128
@@ -423,7 +476,7 @@
     bf16 = jnp.bfloat16
     vmem = pl.BlockSpec(memory_space=pltpu.VMEM)
     return pl.pallas_call(
-        functools.partial(expert_kernel, chips, depth, cap, group),
+        functools.partial(expert_kernel, chips, depth, cap, split, group),
         out_shape=(
             jax.ShapeDtypeStruct((seq_len, width), bf16),
             jax.ShapeDtypeStruct((query_rows, heads * LAT), bf16),
@@ -432,23 +485,23 @@
         out_specs=(vmem, vmem),
         scratch_shapes=[
             pltpu.VMEM((depth, query_rows, lanes), bf16),
-            pltpu.VMEM((chips, cap, width), bf16),
+            pltpu.VMEM((pairs, unit, width), bf16),
             pltpu.VMEM((2, lanes, depth * query_rows), bf16),
             pltpu.VMEM((query_rows, depth * query_rows), jnp.float32),
-            pltpu.VMEM((chips, cap, width), bf16),
+            pltpu.VMEM((pairs, unit, width), bf16),
             pltpu.VMEM((n, tall, width), bf16),
             pltpu.VMEM((2 * n, tall, hidden), bf16),
             pltpu.VMEM((2 * n, tall, hidden), bf16),
             pltpu.VMEM((2 * n, tall, hidden // 2), bf16),
             pltpu.VMEM((n, tall, width), bf16),
-            pltpu.VMEM((chips, cap, width), bf16),
-            pltpu.VMEM((chips, cap, width), bf16),
-            dma((chips,)), dma((chips,)),
-            dma((chips,)), dma((chips,)),
+            pltpu.VMEM((pairs, unit, width), bf16),
+            pltpu.VMEM((pairs, unit, width), bf16),
+            dma((pairs,)), dma((pairs,)),
+            dma((pairs,)), dma((pairs,)),
             dma((2 * n,)), dma((2 * n,)),
             dma((2 * n,)), dma((2 * n,)),
-            dma((chips,)), dma((chips,)),
-            dma((chips,)), dma((chips,)),
+            dma((pairs,)), dma((pairs,)),
+            dma((pairs,)), dma((pairs,)),
             dma((depth,)), dma((depth,)),
         ],
         compiler_params=pltpu.CompilerParams(
@@ -470,7 +523,7 @@
     moe, context = expert_call(
         expert_ids[0].reshape(1, -1),
         features,
-        route_weight[0],
+        route_weight[0].reshape(1, -1),
         w_gate,
         w_up,
         w_down,

time: 134 us -> 129 us (0.963)
  Pallas kernels: 126 us -> 122 us
  local copies, waits for them, and re-layouts: 7.08 us -> 5.54 us
    pallas_call x1, Pallas kernels: 126 us -> 122 us  [expert_call(): pl.pallas_call(functools.partial(expert_kernel, chips, depth, cap, split,...]
    squeeze x1 -> x0, local copies, waits for them, and re-layouts: 1.53 us -> none  [per_device(): route_weight[0]]
where the time goes in v3:
time: 129 us; the launch traced here: 128 us
  Pallas kernels  122 us (95%)
  local copies, waits for them, and re-layouts  5.54 us (4%)
    pallas_call x1, Pallas kernels, expert_call(): pl.pallas_call(functools.partial(expert_kernel, chips, depth, cap, split,...  122 us
    unnamed x5, local copies, waits for them, and re-layouts  5.54 us

profile of v3, /device:TPU:0, one launch (start us, length us, event | category | flops | bytes accessed | tf_op | source)
XLA Modules:
  0.0 128.3 jit_solution(6817800642289720350)
XLA Ops:
  0.6 1.4 %copy.12 = bf16[1,128,64]{2,1,0:T(8,128)(2,1)} copy(bf16[1,128,64]{1,2,0:T(8,128)(2,1)} %param.18) | data formatting | bytes 32768 | tf_op args[8]
  2.1 122.1 %shard_map.113 = (bf16[512,1792]{1,0:T(8,128)(2,1)}, bf16[128,6144]{1,0:T(8,128)(2,1)}) custom-call(s32[1,512]{1,0:T(1,128)} %bitcast.14, bf16[512,1792]{1,0:T(8,128)(2,1)} %bitcast.9, f32[1,512]{1,0:T(1,128)} %bitcast.15, bf16[1792,512]{1,0:T(8,128)(2,1)} %gate_ref.1, bf16[1792,512]{1,0:T(8,128)(2,1)} %up_ref.1, bf16[512,1792]{1,0:T(8,128)(2,1)} %down_ref.1, ...), custom_call_target="tpu_custom_call" | custom-call | tf_op jit(solution)/shard_map/pallas_call | solution.py:478
  124.2 0.0 copy-start
  124.2 3.0 %copy.15 = bf16[1,512,1792]{2,1,0:T(8,128)(2,1)} copy(bf16[1,512,1792]{2,1,0:T(8,128)(2,1)} %bitcast.8) | data formatting | bytes 3670016
  127.2 0.0 copy-done
  127.2 1.1 copy.16
Async XLA Ops:
  124.2 3.0 %copy-start = (bf16[128,6144]{1,0:T(8,128)(2,1)S(1)}, bf16[128,6144]{1,0:T(8,128)(2,1)}, u32[]{:S(2)}) copy-start(bf16[128,6144]{1,0:T(8,128)(2,1)} %get-tuple-element.5) | copy-start | bytes 4718596
